TPU v7x, 128 devices: a whole 4x4x4 slice. The times are simulated.
128 devices in a mesh: row: 8 (over z_lo, y), col: 16 (over x, z_hi, core).
Axes of the slice: x: 4, y: 4, z: 4 (z_hi: 2, z_lo: 2; z = z_hi * 2 + z_lo), core: 2. Of those that a mesh axis runs over, the one named last changes fastest.
Arguments:
- single: bfloat16 [2048, 384], P(('row', 'col')), may hold values from -6 to 6
- pair_input: bfloat16 [2048, 2048, 128], P('row', 'col'), may hold values from -6 to 6
- segment_lengths: int32 [8], replicated, may hold values from 1 to 512, 2048 in all
- single_gain: float32 [384], replicated, may hold values from 0.5 to 1.5
- w_left: bfloat16 [384, 32], replicated, may hold values from -0.3125 to 0.3125
- w_right: bfloat16 [384, 32], replicated, may hold values from -0.3125 to 0.3125
- w_outer: bfloat16 [1024, 128], replicated, may hold values from -0.1875 to 0.1875
- pair_gain: float32 [128], replicated, may hold values from 0.5 to 1.5
- w_gate: bfloat16 [128, 512], replicated, may hold values from -0.5 to 0.5
- w_up: bfloat16 [128, 512], replicated, may hold values from -0.5 to 0.5
- w_down: bfloat16 [512, 128], replicated, may hold values from -0.25 to 0.25
- bias_gain: float32 [128], replicated, may hold values from 0.5 to 1.5
- w_bias: bfloat16 [128, 16], replicated, may hold values from -8 to 8
- w_query: bfloat16 [384, 384], replicated, may hold values from -0.3125 to 0.3125
- w_key: bfloat16 [384, 384], replicated, may hold values from -0.3125 to 0.3125
- w_value: bfloat16 [384, 384], replicated, may hold values from -0.3125 to 0.3125
- w_gate_attn: bfloat16 [384, 384], replicated, may hold values from -0.3125 to 0.3125
- w_output: bfloat16 [384, 384], replicated, may hold values from -0.3125 to 0.3125
Outputs:
- single_out: bfloat16 [2048, 384], P(('row', 'col'))
- pair_out: bfloat16 [2048, 2048, 128], P('row', 'col')
Inputs may be any that keep to these rules, and one draw needn't show every extreme that they name: `segment_lengths`: the last entry is the number of padding tokens at the end of the window; the others are chain lengths.
All inputs are finite; a program needn't handle non-finite values.
Results may differ from a plain program's by a relative error of at most 0.0085.
The roundings to bfloat16 on the way count: a program that leaves them out, or rounds other values in their place, can miss the bound.
Values may be sent and summed in bfloat16 or wider, within the bound.
A program may use at most 128 MiB of HBM per device.

v0:
```python
import math
import jax
import jax.numpy as jnp
from jax import lax
from jax.sharding import PartitionSpec as P

EPSILON = 1e-05


def normalize(values, gain_vector):
    average = jnp.mean(values, -1, keepdims=True)
    centered = values - average
    variance = jnp.mean(centered * centered, -1, keepdims=True)
    return centered * lax.rsqrt(variance + EPSILON) * gain_vector


def matmul(left_side, right_side):
    return jnp.dot(left_side, right_side, preferred_element_type=jnp.float32)


def on_device(
    single,
    pair_input,
    segment_lengths,
    single_gain,
    w_left,
    w_right,
    w_outer,
    pair_gain,
    w_gate,
    w_up,
    w_down,
    bias_gain,
    w_bias,
    w_query,
    w_key,
    w_value,
    w_gate_attn,
    w_output,
):
    row_count = pair_input.shape[0]
    col_count = pair_input.shape[1]
    pair_width = pair_input.shape[2]
    own_count = single.shape[0]
    single_width = single.shape[1]
    head_count = w_bias.shape[1]
    head_dim = single_width // head_count
    outer_width = w_left.shape[1]
    row_devices = lax.axis_size("row")
    row_index = lax.axis_index("row")
    col_index = lax.axis_index("col")
    token_total = row_count * row_devices
    valid_limit = token_total - segment_lengths[segment_lengths.shape[0] - 1]
    row_start = row_index * row_count
    col_start = col_index * col_count

    def alive_mask(first_token, length):
        return (first_token + jnp.arange(length, dtype=jnp.int32) < valid_limit).astype(
            jnp.float32
        )[:, None]

    own_norm = normalize(single.astype(jnp.float32), single_gain).astype(jnp.bfloat16)
    gate_lin = matmul(own_norm, w_gate_attn)
    everything = lax.all_gather(single, ("row", "col"), axis=0, tiled=True)
    row_norm = normalize(
        lax.dynamic_slice_in_dim(everything, row_start, row_count, 0).astype(jnp.float32),
        single_gain,
    ).astype(jnp.bfloat16)
    col_norm = normalize(
        lax.dynamic_slice_in_dim(everything, col_start, col_count, 0).astype(jnp.float32),
        single_gain,
    ).astype(jnp.bfloat16)
    left_rows = (matmul(row_norm, w_left) * alive_mask(row_start, row_count)).astype(jnp.bfloat16)
    query_rows = matmul(row_norm, w_query).astype(jnp.bfloat16)
    right_cols = (matmul(col_norm, w_right) * alive_mask(col_start, col_count)).astype(jnp.bfloat16)
    key_cols = matmul(col_norm, w_key).astype(jnp.bfloat16)
    value_cols = matmul(col_norm, w_value).astype(jnp.bfloat16)
    outer_table = w_outer.reshape(outer_width, outer_width, pair_width)
    right_table = jnp.einsum(
        "jd,cdz->cjz", right_cols, outer_table, preferred_element_type=jnp.float32
    ).astype(jnp.bfloat16)
    right_table = right_table.reshape(outer_width, col_count * pair_width)
    keys_head = key_cols.reshape(col_count, head_count, head_dim)
    values_head = value_cols.reshape(col_count, head_count, head_dim)
    col_alive = col_start + jnp.arange(col_count, dtype=jnp.int32) < valid_limit
    score_scale = 1.0 / math.sqrt(head_dim)
    block_rows = math.gcd(row_count, 32)
    block_total = row_count // block_rows

    def one_block(offset):
        left_block = lax.dynamic_slice_in_dim(left_rows, offset, block_rows, 0)
        pair_block = lax.dynamic_slice_in_dim(pair_input, offset, block_rows, 0)
        middle = pair_block.astype(jnp.float32) + matmul(left_block, right_table).reshape(
            block_rows, col_count, pair_width
        )
        normed = (
            normalize(middle, pair_gain)
            .astype(jnp.bfloat16)
            .reshape(block_rows * col_count, pair_width)
        )
        hidden = (jax.nn.silu(matmul(normed, w_gate)) * matmul(normed, w_up)).astype(jnp.bfloat16)
        new_pair = (
            middle + matmul(hidden, w_down).reshape(block_rows, col_count, pair_width)
        ).astype(jnp.bfloat16)
        bias_input = (
            normalize(new_pair.astype(jnp.float32), bias_gain)
            .astype(jnp.bfloat16)
            .reshape(block_rows * col_count, pair_width)
        )
        pair_bias = matmul(bias_input, w_bias).reshape(block_rows, col_count, head_count)
        query_block = lax.dynamic_slice_in_dim(query_rows, offset, block_rows, 0).reshape(
            block_rows, head_count, head_dim
        )
        scores = (
            jnp.einsum("ihd,jhd->hij", query_block, keys_head, preferred_element_type=jnp.float32)
            * score_scale
        )
        scores = scores + jnp.transpose(pair_bias, (2, 0, 1))
        scores = jnp.where(col_alive[None, None, :], scores, -1e30)
        return (new_pair, scores)

    offsets = jnp.arange(block_total, dtype=jnp.int32) * block_rows
    new_pairs, scores = lax.map(one_block, offsets)
    pair_out = new_pairs.reshape(row_count, col_count, pair_width)
    local_peak = jnp.transpose(jnp.max(scores, -1), (0, 2, 1)).reshape(row_count, head_count)
    row_peak = lax.pmax(local_peak, "col")
    peak_blocks = jnp.transpose(row_peak.reshape(block_total, block_rows, head_count), (0, 2, 1))
    weights = jnp.exp(scores - peak_blocks[..., None])
    denominator = jnp.transpose(jnp.sum(weights, -1), (0, 2, 1)).reshape(row_count, head_count)
    numerator = jnp.einsum(
        "bhij,jhd->bihd",
        weights.astype(jnp.bfloat16),
        values_head,
        preferred_element_type=jnp.float32,
    )
    numerator = numerator.reshape(row_count, single_width)
    numerator, denominator = (
        lax.psum(numerator.astype(jnp.bfloat16), "col").astype(jnp.float32),
        lax.psum(denominator.astype(jnp.bfloat16), "col").astype(jnp.float32),
    )
    own_rows = col_index * own_count
    numerator = lax.dynamic_slice_in_dim(numerator, own_rows, own_count, 0)
    denominator = lax.dynamic_slice_in_dim(denominator, own_rows, own_count, 0)
    attended = (
        numerator.reshape(own_count, head_count, head_dim) / denominator[:, :, None]
    ).reshape(own_count, single_width)
    gated = (jax.nn.sigmoid(gate_lin) * attended).astype(jnp.bfloat16)
    single_out = (single.astype(jnp.float32) + matmul(gated, w_output)).astype(jnp.bfloat16)
    return (single_out, pair_out)


def solution(mesh):
    in_specs = (
        P(("row", "col"), None),
        P("row", "col", None),
        P(),
        P(),
        P(),
        P(),
        P(),
        P(),
        P(),
        P(),
        P(),
        P(),
        P(),
        P(),
        P(),
        P(),
        P(),
        P(),
    )
    out_specs = (P(("row", "col"), None), P("row", "col", None))
    return jax.shard_map(
        on_device, mesh=mesh, in_specs=in_specs, out_specs=out_specs, check_vma=False
    )
```

profile of v0, /device:TPU:0, one launch (start us, length us, event | category | flops | bytes accessed | tf_op | source)
XLA Modules:
  0.0 683.4 jit_solution(7673028879875781972)
XLA Ops:
  12.8 195.2 %all-gather.2.cloned.1.call-done = bf16[2048,384]{1,0:T(8,128)(2,1)} async-done(((bf16[16,384]{1,0:T(8,128)(2,1)}), bf16[2048,384]{1,0:T(8,128)(2,1)}) %all-gather.2.cloned.1.call-update) | async-done | bytes 1572880 | tf_op jit(solution)/shard_map/all_gather | solution.py:64
  221.2 249.4 %while.13 = (s32[]{:T(128)}, bf16[8,32,128,128]{3,2,1,0:T(8,128)(2,1)}, f32[8,16,32,128]{3,2,1,0:T(8,128)}, s32[8]{0:T(128)S(1)}, bf16[256,128,128]{2,1,0:T(8,12...) while((s32[]{:T(128)}, ...), condition=%wide.region_11.12_spmd.clone, body=%wide.region_6.11_spmd.clone.sunk | while | flops 1692082432 | bytes 61893216 | solution.py:123
  225.9 2.1 fusion.117
  228.0 2.4 multiply_reduce_fusion.2
  230.5 2.4 multiply_convert_fusion.3
  232.8 4.5 fusion.118
  237.3 8.0 %fusion.119 = f32[4096,128]{1,0:T(8,128)} fusion(bf16[512,128]{1,0:T(8,128)(2,1)} %get-tuple-element.388, f32[4096,512]{1,0:T(8,128)} %fusion.118, bf16[4096,128]{1,0:T(8,128)(2,1)S(1)} %bitcast.113, bf16[128,512]{1,0:T(8,128)(2,1)} %get-tuple-element.387), kind=kOutput, calls=%fused_computation.13.clone.1 | convolution fusion | flops 1086324736 | bytes 11796480 | tf_op jit(solution)/shard_map/while/body/eval_jaxpr/dot_general | solution.py:18
  245.3 2.5 convert_reduce_fusion.5
  257.0 2.1 fusion.117
  259.1 2.4 multiply_reduce_fusion.2
  261.6 2.4 multiply_convert_fusion.3
  264.0 4.5 fusion.118
  268.4 8.0 %fusion.119 = f32[4096,128]{1,0:T(8,128)} fusion(bf16[512,128]{1,0:T(8,128)(2,1)} %get-tuple-element.388, f32[4096,512]{1,0:T(8,128)} %fusion.118, bf16[4096,128]{1,0:T(8,128)(2,1)S(1)} %bitcast.113, bf16[128,512]{1,0:T(8,128)(2,1)} %get-tuple-element.387), kind=kOutput, calls=%fused_computation.13.clone.1 | convolution fusion | flops 1086324736 | bytes 11796480 | tf_op jit(solution)/shard_map/while/body/eval_jaxpr/dot_general | solution.py:18
  276.5 2.5 convert_reduce_fusion.5
  290.3 2.4 multiply_reduce_fusion.2
  292.7 2.4 multiply_convert_fusion.3
  295.1 4.5 fusion.118
  299.6 8.0 %fusion.119 = f32[4096,128]{1,0:T(8,128)} fusion(bf16[512,128]{1,0:T(8,128)(2,1)} %get-tuple-element.388, f32[4096,512]{1,0:T(8,128)} %fusion.118, bf16[4096,128]{1,0:T(8,128)(2,1)S(1)} %bitcast.113, bf16[128,512]{1,0:T(8,128)(2,1)} %get-tuple-element.387), kind=kOutput, calls=%fused_computation.13.clone.1 | convolution fusion | flops 1086324736 | bytes 11796480 | tf_op jit(solution)/shard_map/while/body/eval_jaxpr/dot_general | solution.py:18
  307.6 2.5 convert_reduce_fusion.5
  321.4 2.4 multiply_reduce_fusion.2
  323.9 2.4 multiply_convert_fusion.3
  326.3 4.5 fusion.118
  330.7 8.0 %fusion.119 = f32[4096,128]{1,0:T(8,128)} fusion(bf16[512,128]{1,0:T(8,128)(2,1)} %get-tuple-element.388, f32[4096,512]{1,0:T(8,128)} %fusion.118, bf16[4096,128]{1,0:T(8,128)(2,1)S(1)} %bitcast.113, bf16[128,512]{1,0:T(8,128)(2,1)} %get-tuple-element.387), kind=kOutput, calls=%fused_computation.13.clone.1 | convolution fusion | flops 1086324736 | bytes 11796480 | tf_op jit(solution)/shard_map/while/body/eval_jaxpr/dot_general | solution.py:18
  338.8 2.5 convert_reduce_fusion.5
  352.6 2.4 multiply_reduce_fusion.2
  355.0 2.4 multiply_convert_fusion.3
  357.4 4.5 fusion.118
  361.9 8.0 %fusion.119 = f32[4096,128]{1,0:T(8,128)} fusion(bf16[512,128]{1,0:T(8,128)(2,1)} %get-tuple-element.388, f32[4096,512]{1,0:T(8,128)} %fusion.118, bf16[4096,128]{1,0:T(8,128)(2,1)S(1)} %bitcast.113, bf16[128,512]{1,0:T(8,128)(2,1)} %get-tuple-element.387), kind=kOutput, calls=%fused_computation.13.clone.1 | convolution fusion | flops 1086324736 | bytes 11796480 | tf_op jit(solution)/shard_map/while/body/eval_jaxpr/dot_general | solution.py:18
  369.9 2.5 convert_reduce_fusion.5
  383.7 2.4 multiply_reduce_fusion.2
  386.2 2.4 multiply_convert_fusion.3
  388.6 4.5 fusion.118
  393.0 8.0 %fusion.119 = f32[4096,128]{1,0:T(8,128)} fusion(bf16[512,128]{1,0:T(8,128)(2,1)} %get-tuple-element.388, f32[4096,512]{1,0:T(8,128)} %fusion.118, bf16[4096,128]{1,0:T(8,128)(2,1)S(1)} %bitcast.113, bf16[128,512]{1,0:T(8,128)(2,1)} %get-tuple-element.387), kind=kOutput, calls=%fused_computation.13.clone.1 | convolution fusion | flops 1086324736 | bytes 11796480 | tf_op jit(solution)/shard_map/while/body/eval_jaxpr/dot_general | solution.py:18
  401.1 2.5 convert_reduce_fusion.5
  414.9 2.4 multiply_reduce_fusion.2
  417.3 2.4 multiply_convert_fusion.3
  419.7 4.5 fusion.118
  424.2 8.0 %fusion.119 = f32[4096,128]{1,0:T(8,128)} fusion(bf16[512,128]{1,0:T(8,128)(2,1)} %get-tuple-element.388, f32[4096,512]{1,0:T(8,128)} %fusion.118, bf16[4096,128]{1,0:T(8,128)(2,1)S(1)} %bitcast.113, bf16[128,512]{1,0:T(8,128)(2,1)} %get-tuple-element.387), kind=kOutput, calls=%fused_computation.13.clone.1 | convolution fusion | flops 1086324736 | bytes 11796480 | tf_op jit(solution)/shard_map/while/body/eval_jaxpr/dot_general | solution.py:18
  432.2 2.5 convert_reduce_fusion.5
  446.0 2.4 multiply_reduce_fusion.2
  448.5 2.4 multiply_convert_fusion.3
  450.9 4.5 fusion.118
  455.3 8.0 %fusion.119 = f32[4096,128]{1,0:T(8,128)} fusion(bf16[512,128]{1,0:T(8,128)(2,1)} %get-tuple-element.388, f32[4096,512]{1,0:T(8,128)} %fusion.118, bf16[4096,128]{1,0:T(8,128)(2,1)S(1)} %bitcast.113, bf16[128,512]{1,0:T(8,128)(2,1)} %get-tuple-element.387), kind=kOutput, calls=%fused_computation.13.clone.1 | convolution fusion | flops 1086324736 | bytes 11796480 | tf_op jit(solution)/shard_map/while/body/eval_jaxpr/dot_general | solution.py:18
  463.4 2.5 convert_reduce_fusion.5
  470.6 2.4 reduce_max.9
  473.0 66.9 %pmax.7 = f32[8,16,32]{2,1,0:T(8,128)S(1)} all-reduce(f32[8,16,32]{2,1,0:T(8,128)S(1)} %reduce_max.9), channel_id=1, replica_groups=mesh['row'=8,'col'=16] {'col'}, use_global_device_ids=true, to_apply=%region_13.14 | all-reduce | flops 4096 | bytes 32768 | tf_op jit(solution)/shard_map/pmax | solution.py:126
  545.7 33.7 %psum.15 = bf16[256,16]{0,1:T(8,128)(2,1)S(1)} all-reduce(bf16[256,16]{0,1:T(8,128)(2,1)S(1)} %convert_element_type.127), channel_id=1, replica_groups=mesh['row'=8,'col'=16] {'col'}, use_global_device_ids=true, to_apply=%region_16.17 | all-reduce | flops 4096 | bytes 16384 | tf_op jit(solution)/shard_map/psum | solution.py:139
  579.8 95.1 %all-reduce.2.cloned.1.call-done = bf16[256,384]{1,0:T(8,128)(2,1)} async-done(((bf16[256,384]{1,0:T(8,128)(2,1)}), bf16[256,384]{1,0:T(8,128)(2,1)}) %all-reduce.2.cloned.1.call-update) | async-done | bytes 196624 | tf_op jit(solution)/shard_map/psum | solution.py:138
  (377 shorter events, 94.6 us)
Async XLA Ops:
  7.2 211.5 %copy-start = (bf16[384,384]{1,0:T(8,128)(2,1)S(1)}, bf16[384,384]{1,0:T(8,128)(2,1)}, u32[]{:S(2)}) copy-start(bf16[384,384]{1,0:T(8,128)(2,1)} %param.33) | copy-start | bytes 884740
  7.2 209.2 %copy-start.9 = (bf16[1024,128]{1,0:T(8,128)(2,1)S(1)}, bf16[1024,128]{1,0:T(8,128)(2,1)}, u32[]{:S(2)}) copy-start(bf16[1024,128]{1,0:T(8,128)(2,1)} %param.26) | copy-start | bytes 786436
  7.2 200.8 %all-gather.2.cloned.1.call-start = ((), (), s32[]{:S(2)}) async-start(), calls=%async_computation | async-start | bytes 1585152 | tf_op jit(solution)/shard_map/all_gather | solution.py:64
  7.9 666.9 %all-reduce.2.cloned.1.call-start = ((), (), s32[]{:S(2)}) async-start(), calls=%async_computation.1 | async-start | bytes 393216 | tf_op jit(solution)/shard_map/psum | solution.py:138
  214.4 4.4 copy-start.15
  216.4 3.6 copy-start.20
  245.3 3.9 copy-start.21
  245.3 3.9 copy-start.22
  252.5 3.5 copy-start.1
  252.6 3.5 copy-start.11
  252.6 3.5 copy-start.23
  276.4 3.9 copy-start.21
  276.5 3.9 copy-start.22
  283.7 3.5 copy-start.1
  283.7 3.5 copy-start.11
  283.7 3.5 copy-start.23
  307.6 3.9 copy-start.21
  307.6 3.9 copy-start.22
  314.8 3.5 copy-start.1
  314.9 3.5 copy-start.11
  314.9 3.5 copy-start.23
  338.7 3.9 copy-start.21
  338.8 3.9 copy-start.22
  346.0 3.5 copy-start.1
  346.0 3.5 copy-start.11
  346.0 3.5 copy-start.23
  369.9 3.9 copy-start.21
  369.9 3.9 copy-start.22
  377.1 3.5 copy-start.1
  377.1 3.5 copy-start.11
  377.2 3.5 copy-start.23
  401.0 3.9 copy-start.21
  401.0 3.9 copy-start.22
  408.3 3.5 copy-start.11
  408.3 3.5 copy-start.23
  432.2 3.9 copy-start.21
  432.2 3.9 copy-start.22
  439.4 3.5 copy-start.11
  439.5 3.5 copy-start.23
  463.3 3.9 copy-start.21
  463.3 3.9 copy-start.22
  470.6 69.3 %copy-start.3 = (f32[8,16,32,128]{3,2,1,0:T(8,128)S(1)}, f32[8,16,32,128]{3,2,1,0:T(8,128)}, u32[]{:S(2)}) copy-start(f32[8,16,32,128]{3,2,1,0:T(8,128)} %get-tuple-element.85) | copy-start | bytes 6291460
  473.0 68.2 %copy-start.6 = (bf16[128,384]{0,1:T(8,128)(2,1)S(1)}, bf16[128,384]{0,1:T(8,128)(2,1)}, u32[]{:S(2)}) copy-start(bf16[128,384]{0,1:T(8,128)(2,1)} %copy.42) | copy-start | bytes 294916
  542.7 132.2 %copy-start.7 = (bf16[384,384]{1,0:T(8,128)(2,1)S(1)}, bf16[384,384]{1,0:T(8,128)(2,1)}, u32[]{:S(2)}) copy-start(bf16[384,384]{1,0:T(8,128)(2,1)} %param.37) | copy-start | bytes 884740
  542.7 132.2 %copy-start.8 = (bf16[384,384]{1,0:T(8,128)(2,1)S(1)}, bf16[384,384]{1,0:T(8,128)(2,1)}, u32[]{:S(2)}) copy-start(bf16[384,384]{1,0:T(8,128)(2,1)} %param.36) | copy-start | bytes 884740
  542.7 132.1 %copy-start.10 = (bf16[16,384]{1,0:T(8,128)(2,1)S(1)}, bf16[16,384]{1,0:T(8,128)(2,1)}, u32[]{:S(2)}) copy-start(bf16[16,384]{1,0:T(8,128)(2,1)} %param.20) | copy-start | bytes 36868
  542.7 132.1 %copy-start.16 = (f32[384]{0:T(512)S(1)}, f32[384]{0:T(512)}, u32[]{:S(2)}) copy-start(f32[384]{0:T(512)} %param.23) | copy-start | bytes 4612
  542.7 132.1 %copy-start.18 = (f32[16]{0:T(128)S(1)}, f32[16]{0:T(128)}, u32[]{:S(2)}) copy-start(f32[16]{0:T(128)} %copy-done.17) | copy-start | bytes 196
  (63 other events, 182.1 us)
Sparse Core Ops, SparseCore 0:
  9.7 198.2 all-gather.1
  545.7 129.0 all-reduce.1
where the time goes:
time: 685 us; the launch traced here: 683 us
  waiting for transfers between devices  291 us (42%)
  matrix products  132 us (19%)
  other arithmetic  101 us (15%)
  blocking collectives  101 us (15%)
  local copies, waits for them, and re-layouts  26.2 us (4%)
  loops' own time  18.1 us (3%)
  between operations  15 us (2%)
    all_gather x1, waiting for transfers between devices, on_device(): everything = lax.all_gather(single, ('row', 'col'), axis=0, tiled=True)  195 us
    dot_general x37, matrix products, matmul(): return jnp.dot(left_side, right_side, preferred_element_type=jnp.float32)  121 us
    psum x1, waiting for transfers between devices, on_device(): lax.psum(numerator.astype(jnp.bfloat16), 'col').astype(jnp.float32)  95.1 us
    pmax x1, blocking collectives, on_device(): row_peak = lax.pmax(local_peak, 'col')  66.9 us
    reduce_sum x19, other arithmetic, normalize(): average = jnp.mean(values, -1, keepdims=True)  39.9 us
    psum x1, blocking collectives, on_device(): lax.psum(denominator.astype(jnp.bfloat16), 'col').astype(jnp.float32)  33.7 us
    reduce_sum x19, other arithmetic, normalize(): variance = jnp.mean(centered * centered, -1, keepdims=True)  33.2 us
    convert_element_type x8, other arithmetic, one_block(): normed = normalize(middle, pair_gain).astype(jnp.bfloat16).reshape(block_...  19 us
  transfers between devices with their start and end apart: 2, of which 2 were waited for; matrix products, arithmetic and copies ran while one was open for 1% of the time, Pallas kernels for 0%

commit v1 on v0

--- a/solution.py
+++ b/solution.py
@@ -61,7 +61,8 @@
 
     own_norm = normalize(single.astype(jnp.float32), single_gain).astype(jnp.bfloat16)
     gate_lin = matmul(own_norm, w_gate_attn)
-    everything = lax.all_gather(single, ("row", "col"), axis=0, tiled=True)
+    sent = jnp.stack([single] * lax.axis_size(("row", "col")))
+    everything = jnp.concatenate(lax.all_to_all(sent, ("row", "col"), 0, 0), axis=0)
     row_norm = normalize(
         lax.dynamic_slice_in_dim(everything, row_start, row_count, 0).astype(jnp.float32),
         single_gain,

time: 685 us -> 515 us (0.75)
  waiting for transfers between devices: 291 us -> 115 us
  starting transfers between devices: 0.08 us -> 11.2 us
    all_gather x1 -> x0, waiting for transfers between devices: 195 us -> none  [on_device(): everything = lax.all_gather(single, ('row', 'col'), axis=0, tiled=True)]
    all_to_all x0 -> x1, waiting for transfers between devices: none -> 20.8 us  [on_device(): lax.all_to_all(sent, ('row', 'col'), 0, 0)]
    all_to_all x0 -> x1, starting transfers between devices: none -> 11.2 us  [on_device(): lax.all_to_all(sent, ('row', 'col'), 0, 0)]
  transfers between devices with their start and end apart: 2 -> 2, of which waited for: 2 -> 2; matrix products, arithmetic and copies ran while one was open for 1% -> 0% of each run, Pallas kernels for 0% -> 0%
where the time goes in v1:
time: 515 us; the launch traced here: 513 us
  matrix products  130 us (25%)
  waiting for transfers between devices  115 us (22%)
  blocking collectives  101 us (20%)
  other arithmetic  95.3 us (19%)
  local copies, waits for them, and re-layouts  27 us (5%)
  loops' own time  18.3 us (4%)
  between operations  15.1 us (3%)
  starting transfers between devices  11.2 us (2%)
    dot_general x37, matrix products, matmul(): return jnp.dot(left_side, right_side, preferred_element_type=jnp.float32)  119 us
    psum x1, waiting for transfers between devices, on_device(): lax.psum(numerator.astype(jnp.bfloat16), 'col').astype(jnp.float32)  94.6 us
    pmax x1, blocking collectives, on_device(): row_peak = lax.pmax(local_peak, 'col')  67.5 us
    reduce_sum x19, other arithmetic, normalize(): average = jnp.mean(values, -1, keepdims=True)  37.4 us
    psum x1, blocking collectives, on_device(): lax.psum(denominator.astype(jnp.bfloat16), 'col').astype(jnp.float32)  33.7 us
    reduce_sum x19, other arithmetic, normalize(): variance = jnp.mean(centered * centered, -1, keepdims=True)  30.6 us
    all_to_all x1, waiting for transfers between devices, on_device(): lax.all_to_all(sent, ('row', 'col'), 0, 0)  20.8 us
    convert_element_type x8, other arithmetic, one_block(): normed = normalize(middle, pair_gain).astype(jnp.bfloat16).reshape(block_...  19 us
  transfers between devices with their start and end apart: 2, of which 2 were waited for; matrix products, arithmetic and copies ran while one was open for 0% of the time, Pallas kernels for 0%

profile of v1, /device:TPU:0, one launch (start us, length us, event | category | flops | bytes accessed | tf_op | source)
XLA Modules:
  0.0 513.3 jit_solution(5963061855101235303)
XLA Ops:
  9.3 11.2 %all-to-all-start = ((bf16[128,16,384]{2,1,0:T(8,128)(2,1)}), bf16[128,16,384]{2,1,0:T(8,128)(2,1)S(1)}, u32[]{:S(2)}, u32[]{:S(2)}) async-start(bf16[128,16,384]{2,1,0:T(8,128)(2,1)} %stack.2), calls=%async_computation | async-start | bytes 3145728 | tf_op jit(solution)/shard_map/all_to_all | solution.py:65
  22.7 20.8 %all-to-all-done = bf16[128,16,384]{2,1,0:T(8,128)(2,1)S(1)} async-done(((bf16[128,16,384]{2,1,0:T(8,128)(2,1)}), bf16[128,16,384]{2,1,0:T(8,128)(2,1)S(1)}, u32[]{:S(2)}, u32[]{:S(2)}) %all-to-all-start) | async-done | bytes 1572896 | tf_op jit(solution)/shard_map/all_to_all | solution.py:65
  51.1 249.3 %while.13 = (s32[]{:T(128)}, bf16[8,32,128,128]{3,2,1,0:T(8,128)(2,1)}, f32[8,16,32,128]{3,2,1,0:T(8,128)}, s32[8]{0:T(128)S(1)}, bf16[256,128,128]{2,1,0:T(8,12...) while((s32[]{:T(128)}, ...), condition=%wide.region_11.12_spmd.clone, body=%wide.region_6.11_spmd.clone.sunk | while | flops 1692082432 | bytes 62022272 | solution.py:124
  55.7 2.1 fusion.117
  57.8 2.4 multiply_reduce_fusion.2
  60.3 2.4 multiply_convert_fusion.3
  62.7 4.5 fusion.118
  67.1 8.0 %fusion.119 = f32[4096,128]{1,0:T(8,128)} fusion(bf16[512,128]{1,0:T(8,128)(2,1)} %get-tuple-element.405, f32[4096,512]{1,0:T(8,128)} %fusion.118, bf16[4096,128]{1,0:T(8,128)(2,1)S(1)} %bitcast.114, bf16[128,512]{1,0:T(8,128)(2,1)} %get-tuple-element.404), kind=kOutput, calls=%fused_computation.13.clone.1 | convolution fusion | flops 1086324736 | bytes 11796480 | tf_op jit(solution)/shard_map/while/body/eval_jaxpr/dot_general | solution.py:18
  75.2 2.5 convert_reduce_fusion.5
  89.0 2.4 multiply_reduce_fusion.2
  91.4 2.4 multiply_convert_fusion.3
  93.8 4.5 fusion.118
  98.3 8.0 %fusion.119 = f32[4096,128]{1,0:T(8,128)} fusion(bf16[512,128]{1,0:T(8,128)(2,1)} %get-tuple-element.405, f32[4096,512]{1,0:T(8,128)} %fusion.118, bf16[4096,128]{1,0:T(8,128)(2,1)S(1)} %bitcast.114, bf16[128,512]{1,0:T(8,128)(2,1)} %get-tuple-element.404), kind=kOutput, calls=%fused_computation.13.clone.1 | convolution fusion | flops 1086324736 | bytes 11796480 | tf_op jit(solution)/shard_map/while/body/eval_jaxpr/dot_general | solution.py:18
  106.3 2.5 convert_reduce_fusion.5
  120.1 2.4 multiply_reduce_fusion.2
  122.5 2.4 multiply_convert_fusion.3
  124.9 4.5 fusion.118
  129.4 8.0 %fusion.119 = f32[4096,128]{1,0:T(8,128)} fusion(bf16[512,128]{1,0:T(8,128)(2,1)} %get-tuple-element.405, f32[4096,512]{1,0:T(8,128)} %fusion.118, bf16[4096,128]{1,0:T(8,128)(2,1)S(1)} %bitcast.114, bf16[128,512]{1,0:T(8,128)(2,1)} %get-tuple-element.404), kind=kOutput, calls=%fused_computation.13.clone.1 | convolution fusion | flops 1086324736 | bytes 11796480 | tf_op jit(solution)/shard_map/while/body/eval_jaxpr/dot_general | solution.py:18
  137.4 2.5 convert_reduce_fusion.5
  151.2 2.4 multiply_reduce_fusion.2
  153.7 2.4 multiply_convert_fusion.3
  156.1 4.5 fusion.118
  160.5 8.0 %fusion.119 = f32[4096,128]{1,0:T(8,128)} fusion(bf16[512,128]{1,0:T(8,128)(2,1)} %get-tuple-element.405, f32[4096,512]{1,0:T(8,128)} %fusion.118, bf16[4096,128]{1,0:T(8,128)(2,1)S(1)} %bitcast.114, bf16[128,512]{1,0:T(8,128)(2,1)} %get-tuple-element.404), kind=kOutput, calls=%fused_computation.13.clone.1 | convolution fusion | flops 1086324736 | bytes 11796480 | tf_op jit(solution)/shard_map/while/body/eval_jaxpr/dot_general | solution.py:18
  168.5 2.5 convert_reduce_fusion.5
  182.4 2.4 multiply_reduce_fusion.2
  184.8 2.4 multiply_convert_fusion.3
  187.2 4.5 fusion.118
  191.7 8.0 %fusion.119 = f32[4096,128]{1,0:T(8,128)} fusion(bf16[512,128]{1,0:T(8,128)(2,1)} %get-tuple-element.405, f32[4096,512]{1,0:T(8,128)} %fusion.118, bf16[4096,128]{1,0:T(8,128)(2,1)S(1)} %bitcast.114, bf16[128,512]{1,0:T(8,128)(2,1)} %get-tuple-element.404), kind=kOutput, calls=%fused_computation.13.clone.1 | convolution fusion | flops 1086324736 | bytes 11796480 | tf_op jit(solution)/shard_map/while/body/eval_jaxpr/dot_general | solution.py:18
  199.7 2.5 convert_reduce_fusion.5
  213.5 2.4 multiply_reduce_fusion.2
  215.9 2.4 multiply_convert_fusion.3
  218.3 4.5 fusion.118
  222.8 8.0 %fusion.119 = f32[4096,128]{1,0:T(8,128)} fusion(bf16[512,128]{1,0:T(8,128)(2,1)} %get-tuple-element.405, f32[4096,512]{1,0:T(8,128)} %fusion.118, bf16[4096,128]{1,0:T(8,128)(2,1)S(1)} %bitcast.114, bf16[128,512]{1,0:T(8,128)(2,1)} %get-tuple-element.404), kind=kOutput, calls=%fused_computation.13.clone.1 | convolution fusion | flops 1086324736 | bytes 11796480 | tf_op jit(solution)/shard_map/while/body/eval_jaxpr/dot_general | solution.py:18
  230.8 2.5 convert_reduce_fusion.5
  244.7 2.4 multiply_reduce_fusion.2
  247.1 2.4 multiply_convert_fusion.3
  249.5 4.5 fusion.118
  254.0 8.0 %fusion.119 = f32[4096,128]{1,0:T(8,128)} fusion(bf16[512,128]{1,0:T(8,128)(2,1)} %get-tuple-element.405, f32[4096,512]{1,0:T(8,128)} %fusion.118, bf16[4096,128]{1,0:T(8,128)(2,1)S(1)} %bitcast.114, bf16[128,512]{1,0:T(8,128)(2,1)} %get-tuple-element.404), kind=kOutput, calls=%fused_computation.13.clone.1 | convolution fusion | flops 1086324736 | bytes 11796480 | tf_op jit(solution)/shard_map/while/body/eval_jaxpr/dot_general | solution.py:18
  262.0 2.5 convert_reduce_fusion.5
  275.8 2.4 multiply_reduce_fusion.2
  278.2 2.4 multiply_convert_fusion.3
  280.6 4.5 fusion.118
  285.1 8.0 %fusion.119 = f32[4096,128]{1,0:T(8,128)} fusion(bf16[512,128]{1,0:T(8,128)(2,1)} %get-tuple-element.405, f32[4096,512]{1,0:T(8,128)} %fusion.118, bf16[4096,128]{1,0:T(8,128)(2,1)S(1)} %bitcast.114, bf16[128,512]{1,0:T(8,128)(2,1)} %get-tuple-element.404), kind=kOutput, calls=%fused_computation.13.clone.1 | convolution fusion | flops 1086324736 | bytes 11796480 | tf_op jit(solution)/shard_map/while/body/eval_jaxpr/dot_general | solution.py:18
  293.1 2.5 convert_reduce_fusion.5
  300.4 2.4 reduce_max.9
  302.7 67.5 %pmax.7 = f32[8,16,32]{2,1,0:T(8,128)S(1)} all-reduce(f32[8,16,32]{2,1,0:T(8,128)S(1)} %reduce_max.9), channel_id=1, replica_groups=mesh['row'=8,'col'=16] {'col'}, use_global_device_ids=true, to_apply=%region_13.14 | all-reduce | flops 4096 | bytes 32768 | tf_op jit(solution)/shard_map/pmax | solution.py:127
  376.1 33.7 %psum.15 = bf16[256,16]{0,1:T(8,128)(2,1)S(1)} all-reduce(bf16[256,16]{0,1:T(8,128)(2,1)S(1)} %convert_element_type.127), channel_id=1, replica_groups=mesh['row'=8,'col'=16] {'col'}, use_global_device_ids=true, to_apply=%region_16.17 | all-reduce | flops 4096 | bytes 16384 | tf_op jit(solution)/shard_map/psum | solution.py:140
  410.1 94.6 %all-reduce.2.cloned.1.call-done = bf16[256,384]{1,0:T(8,128)(2,1)} async-done(((bf16[256,384]{1,0:T(8,128)(2,1)}), bf16[256,384]{1,0:T(8,128)(2,1)}) %all-reduce.2.cloned.1.call-update) | async-done | bytes 196624 | tf_op jit(solution)/shard_map/psum | solution.py:139
  (405 shorter events, 89.4 us)
Async XLA Ops:
  7.2 41.4 %copy-start = (bf16[384,384]{1,0:T(8,128)(2,1)S(1)}, bf16[384,384]{1,0:T(8,128)(2,1)}, u32[]{:S(2)}) copy-start(bf16[384,384]{1,0:T(8,128)(2,1)} %param.33) | copy-start | bytes 884740
  7.2 14.7 %copy-start.11 = (bf16[16,384]{1,0:T(8,128)(2,1)S(1)}, bf16[16,384]{1,0:T(8,128)(2,1)}, u32[]{:S(2)}) copy-start(bf16[16,384]{1,0:T(8,128)(2,1)} %param.20) | copy-start | bytes 36868
  7.2 13.3 %copy-start.28 = (s32[8]{0:T(128)S(1)}, s32[8]{0:T(128)}, u32[]{:S(2)}) copy-start(s32[8]{0:T(128)} %param.22) | copy-start | bytes 100
  9.2 35.0 %copy-start.19 = (f32[384]{0:T(512)S(1)}, f32[384]{0:T(512)}, u32[]{:S(2)}) copy-start(f32[384]{0:T(512)} %param.23) | copy-start | bytes 4612
  9.3 35.0 %copy-start.24 = (bf16[384,384]{1,0:T(8,128)(2,1)S(1)}, bf16[384,384]{1,0:T(8,128)(2,1)}, u32[]{:S(2)}) copy-start(bf16[384,384]{1,0:T(8,128)(2,1)} %param.34) | copy-start | bytes 884740
  9.3 36.0 %copy-start.25 = (bf16[384,384]{1,0:T(8,128)(2,1)S(1)}, bf16[384,384]{1,0:T(8,128)(2,1)}, u32[]{:S(2)}) copy-start(bf16[384,384]{1,0:T(8,128)(2,1)} %param.35) | copy-start | bytes 884740
  9.3 37.0 %copy-start.10 = (bf16[1024,128]{1,0:T(8,128)(2,1)S(1)}, bf16[1024,128]{1,0:T(8,128)(2,1)}, u32[]{:S(2)}) copy-start(bf16[1024,128]{1,0:T(8,128)(2,1)} %param.26) | copy-start | bytes 786436
  9.3 37.0 %copy-start.16 = (bf16[384,32]{0,1:T(8,128)(2,1)S(1)}, bf16[384,32]{0,1:T(8,128)(2,1)}, u32[]{:S(2)}) copy-start(bf16[384,32]{0,1:T(8,128)(2,1)} %param.25) | copy-start | bytes 73732
  9.3 34.3 %all-to-all-start = ((bf16[128,16,384]{2,1,0:T(8,128)(2,1)}), bf16[128,16,384]{2,1,0:T(8,128)(2,1)S(1)}, u32[]{:S(2)}, u32[]{:S(2)}) async-start(bf16[128,16,384]{2,1,0:T(8,128)(2,1)} %stack.2), calls=%async_computation | async-start | bytes 3145728 | tf_op jit(solution)/shard_map/all_to_all | solution.py:65
  20.5 484.3 %all-reduce.2.cloned.1.call-start = ((), (), s32[]{:S(2)}) async-start(), calls=%async_computation.1 | async-start | bytes 393216 | tf_op jit(solution)/shard_map/psum | solution.py:139
  22.0 21.8 %copy-start.21 = (f32[16]{0:T(128)}, f32[16]{0:T(128)S(1)}, u32[]{:S(2)}) copy-start(f32[16]{0:T(128)S(1)} %broadcast_multiply_fusion.4) | copy-start | bytes 196
  46.3 3.6 copy-start.26
  46.3 4.8 copy-start.17
  51.3 3.5 copy-start.1
  75.1 3.9 copy-start.27
  75.1 3.9 copy-start.29
  82.4 3.5 copy-start.1
  82.4 3.5 copy-start.12
  82.4 3.5 copy-start.14
  82.4 3.5 copy-start.30
  106.3 3.9 copy-start.27
  106.3 3.9 copy-start.29
  113.5 3.5 copy-start.1
  113.5 3.5 copy-start.12
  113.6 3.5 copy-start.14
  137.4 3.9 copy-start.27
  137.4 3.9 copy-start.29
  144.7 3.5 copy-start.1
  168.5 3.9 copy-start.27
  168.5 3.9 copy-start.29
  175.8 3.5 copy-start.1
  199.7 3.9 copy-start.27
  199.7 3.9 copy-start.29
  206.9 3.5 copy-start.1
  230.8 3.9 copy-start.27
  230.8 3.9 copy-start.29
  238.1 3.5 copy-start.1
  262.0 3.9 copy-start.27
  262.0 3.9 copy-start.29
  269.2 3.5 copy-start.1
  293.1 3.9 copy-start.27
  293.1 3.9 copy-start.29
  300.4 69.9 %copy-start.3 = (f32[8,16,32,128]{3,2,1,0:T(8,128)S(1)}, f32[8,16,32,128]{3,2,1,0:T(8,128)}, u32[]{:S(2)}) copy-start(f32[8,16,32,128]{3,2,1,0:T(8,128)} %get-tuple-element.85) | copy-start | bytes 6291460
  302.7 68.8 %copy-start.7 = (bf16[128,384]{0,1:T(8,128)(2,1)S(1)}, bf16[128,384]{0,1:T(8,128)(2,1)}, u32[]{:S(2)}) copy-start(bf16[128,384]{0,1:T(8,128)(2,1)} %copy.52) | copy-start | bytes 294916
  373.0 131.7 %copy-start.8 = (bf16[384,384]{1,0:T(8,128)(2,1)S(1)}, bf16[384,384]{1,0:T(8,128)(2,1)}, u32[]{:S(2)}) copy-start(bf16[384,384]{1,0:T(8,128)(2,1)} %param.37) | copy-start | bytes 884740
  373.1 131.7 %copy-start.9 = (bf16[384,384]{1,0:T(8,128)(2,1)S(1)}, bf16[384,384]{1,0:T(8,128)(2,1)}, u32[]{:S(2)}) copy-start(bf16[384,384]{1,0:T(8,128)(2,1)} %param.36) | copy-start | bytes 884740
  373.1 131.7 %copy-start.20 = (f32[384]{0:T(512)S(1)}, f32[384]{0:T(512)}, u32[]{:S(2)}) copy-start(f32[384]{0:T(512)} %param.23) | copy-start | bytes 4612
  373.1 131.7 %copy-start.22 = (f32[16]{0:T(128)S(1)}, f32[16]{0:T(128)}, u32[]{:S(2)}) copy-start(f32[16]{0:T(128)} %copy-done.21) | copy-start | bytes 196
  (77 other events, 240.0 us)
Sparse Core Ops, SparseCore 0:
  376.0 128.6 all-reduce.1
